TPU v7x, 128 devices: a whole 4x4x4 slice. The times are simulated.
128 devices in a mesh: freq: 4 (over z_lo, core), facet: 32 (over y, x, z_hi).
Axes of the slice: x: 4, y: 4, z: 4 (z_hi: 2, z_lo: 2; z = z_hi * 2 + z_lo), core: 2. Of those that a mesh axis runs over, the one named last changes fastest.
Arguments:
- visibilities: float32 [64, 2, 2048], P('facet', None, 'freq'), may hold values from -6 to 6
- weights: float32 [64, 2048], P('facet', 'freq'), may hold values from 0.1 to 1
- uv_cells: int32 [64, 2, 2048], P('facet', None, 'freq'), may hold values from -16384 to 16383
- flags: int32 [64, 2048], P('facet', 'freq'), may hold values from 0 to 1, as said below
- plan: int32 [64], replicated, may hold values from 0 to 63, each once
- beam: float32 [32, 64], P('facet'), may hold values from 0.2 to 1
- facets: int32 [32, 2], P('facet'), may hold values from 0 to 255
Outputs:
- dirty_image: float32 [32, 128, 128], P('facet', 'freq')
Inputs may be any that keep to these rules, and one draw needn't show every extreme that they name: `flags`: in each block, each frequency group's 512 rows hold at most 256 unflagged rows; in every draw some block holds exactly 256 in every group. `plan`: each of the 64 blocks is read at exactly one step.
All inputs are finite; a program needn't handle non-finite values.
Results may differ from a plain program's by a relative error of at most 0.0037.
Values sent between devices are 32-bit elements; how exact they have to be, the bound alone decides.
No kernel may reach another device: no remote copies, remote signals or barrier semaphores. Data moves between devices by JAX's collectives and lax.ppermute only.
A program may use at most 64 MiB of HBM per device.

v0:
```python
import math
import jax
import jax.numpy as jnp
from jax import lax
from jax.sharding import PartitionSpec as P

P_SIZE = 128
IMG = 32768
full_turn = 2.0 * math.pi
slab_limit = 16384
fine_count = 16


def angle_table(factors, cells):
    turns = jnp.mod(factors[:, None] * cells[None, :], IMG).astype(jnp.float32) * (full_turn / IMG)
    return (jnp.cos(turns), jnp.sin(turns))


def phase_table(base, cells):
    coarse_count = P_SIZE // fine_count
    base_cos, base_sin = angle_table(jnp.reshape(base, (1,)), cells)
    coarse_cos, coarse_sin = angle_table(
        jnp.arange(coarse_count, dtype=jnp.int32) * fine_count, cells
    )
    fine_cos, fine_sin = angle_table(jnp.arange(fine_count, dtype=jnp.int32), cells)
    outer_cos = base_cos * coarse_cos - base_sin * coarse_sin
    outer_sin = base_sin * coarse_cos + base_cos * coarse_sin
    full_cos = (
        outer_cos[:, None, :] * fine_cos[None, :, :] - outer_sin[:, None, :] * fine_sin[None, :, :]
    )
    full_sin = (
        outer_sin[:, None, :] * fine_cos[None, :, :] + outer_cos[:, None, :] * fine_sin[None, :, :]
    )
    extent = cells.shape[0]
    return (full_cos.reshape(P_SIZE, extent), full_sin.reshape(P_SIZE, extent))


def facet_image(samples, facet_col, facet_row):
    u_cells = samples[3].astype(jnp.int32)
    v_cells = samples[4].astype(jnp.int32)
    cos_u, sin_u = phase_table(facet_col * P_SIZE - IMG // 2, u_cells)
    real_part = samples[0] * samples[2]
    imag_part = samples[1] * samples[2]
    left = jnp.concatenate(
        [real_part * cos_u - imag_part * sin_u, -(real_part * sin_u + imag_part * cos_u)], axis=1
    ).astype(jnp.bfloat16)
    cos_v, sin_v = phase_table(facet_row * P_SIZE - IMG // 2, v_cells)
    right = jnp.concatenate([cos_v, sin_v], axis=1).astype(jnp.bfloat16)
    return lax.dot_general(
        left, right, (((1,), (1,)), ((), ())), preferred_element_type=jnp.float32
    )


def slab_image(samples, facet_col, facet_row):
    extent = samples.shape[1]
    slabs = samples.reshape(5, extent // slab_limit, slab_limit).transpose(1, 0, 2)

    def advance(running, slab):
        return (running + facet_image(slab, facet_col, facet_row), None)

    summed, _ = lax.scan(advance, jnp.zeros((P_SIZE, P_SIZE), jnp.float32), slabs)
    return summed


def flatten_blocks(packed, factors):
    scaled = packed[:, 2, :] * factors[:, None]
    joined = jnp.concatenate([packed[:, :2, :], scaled[:, None, :], packed[:, 3:, :]], axis=1)
    return joined.transpose(1, 0, 2).reshape(5, -1)


def body(visibilities, weights, uv_cells, flags, plan, beam, facets):
    live = weights * flags.astype(jnp.float32)
    packed = jnp.concatenate([visibilities, live[:, None, :], uv_cells.astype(jnp.float32)], axis=1)
    total_blocks = plan.shape[0]
    matches = (plan[:, None] == jnp.arange(total_blocks, dtype=jnp.int32)[None, :]).astype(
        jnp.float32
    )
    gains = jnp.sum(beam[0][:, None] * matches, axis=0)
    facet_col = facets[0, 0]
    facet_row = facets[0, 1]
    image = slab_image(
        flatten_blocks(lax.all_gather(packed, "facet", axis=0, tiled=True), gains),
        facet_col,
        facet_row,
    )
    share = lax.psum_scatter(image, "freq", scatter_dimension=0, tiled=True)
    scale = 2.0 / math.sqrt(total_blocks * weights.shape[1] * lax.axis_size("freq"))
    return (share * scale)[None]


def solution(mesh):
    in_specs = (
        P("facet", None, "freq"),
        P("facet", "freq"),
        P("facet", None, "freq"),
        P("facet", "freq"),
        P(),
        P("facet", None),
        P("facet", None),
    )
    out_specs = P("facet", "freq", None)
    return jax.shard_map(body, mesh=mesh, in_specs=in_specs, out_specs=out_specs, check_vma=False)
```

profile of v0, /device:TPU:1, one launch (start us, length us, event | category | flops | bytes accessed | tf_op | source)
XLA Modules:
  0.0 203.0 jit_solution(12933893324455298943)
XLA Ops:
  6.5 0.0 reduce-scatter.2.cloned.1.call-start
  6.5 0.7 convert_multiply_fusion
  7.3 0.7 convert_element_type.174
  8.0 0.7 pad_maximum_fusion.1
  8.7 88.1 %all_gather.3 = f32[64,5,512]{2,1,0:T(8,128)S(1)} all-gather(f32[2,5,512]{2,1,0:T(8,128)S(1)} %pad_maximum_fusion.1), channel_id=1, replica_groups=mesh['freq'=4,'facet'=32] {'facet'}, dimensions={0}, use_global_device_ids=true | all-gather | bytes 675840 | tf_op jit(solution)/shard_map/all_gather | solution.py:82
  96.7 0.2 fusion.54
  96.9 0.8 select_reduce_fusion
  97.7 0.2 slice_multiply_fusion
  97.9 1.3 fusion.55
  100.5 0.3 pad_maximum_fusion
  100.8 67.1 %while.14 = (s32[]{:T(128)}, f32[128,128]{1,0:T(8,128)S(1)}, f32[2,5,16384]{2,1,0:T(8,128)S(1)}, s32[]{:T(128)}, s32[]{:T(128)}, /*index=5*/s32[]{:T(128)}, s32[]{:T(128)}, s32[]{}, s32[]{}, s32[]{}, /*index=10*/s32[]{}) while((s32[]{:T(128)}, f32[128,128]{1,0:T(8,128)S(1)}, f32[2,5,16384]{2,1,0:T(8,128)S(1)}, s32[]{:T(128)}, ...), condition=%wide.region_2.3_spmd.clone, body=%wide.region_1.2_spmd.clone.sunk | while | flops 1168670720 | bytes 81461504 | solution.py:61
  100.9 0.3 dynamic-slice_multiply_fusion.3
  101.1 0.5 fusion.66
  101.7 4.3 %multiply_subtract_fusion.5 = (f32[8,16384]{1,0:T(8,128)S(1)}, f32[8,16384]{1,0:T(8,128)S(1)}, f32[8,16384]{1,0:T(8,128)S(1)}, f32[8,16384]{1,0:T(8,128)S(1)}) fusion(f32[16384]{0:T(1024)S(1)} %get-tuple-element.221, s32[16384]{0:T(1024)S(1)} %bitcast.58, s32[8]{0:T(128)S(1)} %iota_multiply_fusion.2, f32[16384]{0:T(1024)S(1)} %get-tuple-element.222, ...), kind=kLoop, calls=%fused_computation.62.clone.1 | loop fusion | flops 5242880 | bytes 2490400 | tf_op jit(solution)/shard_map/while/body/eval_jaxpr/sub | solution.py:26
  106.0 4.1 %fusion.67 = (f32[16,16384]{1,0:T(8,128)S(1)}, f32[16,16384]{1,0:T(8,128)S(1)}) fusion(s32[16384]{0:T(1024)S(1)} %bitcast.59), kind=kLoop, calls=%fused_computation.61.clone.1 | loop fusion | flops 3670016 | bytes 2162688 | tf_op jit(solution)/shard_map/while/body/eval_jaxpr/cos | solution.py:16
  110.1 2.3 %multiply_subtract_fusion.6 = (f32[8,16,16384]{2,1,0:T(8,128)S(1)}, f32[8,16,16384]{2,1,0:T(8,128)S(1)}) fusion(f32[16,16384]{1,0:T(8,128)S(1)} %get-tuple-element.230, f32[8,16384]{1,0:T(8,128)S(1)} %get-tuple-element.231, f32[16,16384]{1,0:T(8,128)S(1)} %get-tuple-element.232, f32[8,16384]{1,0:T(8,128)S(1)} %get-tuple-element.233), kind=kLoop, calls=%fused_computation.19.clone.1 | loop fusion | flops 12582912 | bytes 19922944 | tf_op jit(solution)/shard_map/while/body/eval_jaxpr/sub | solution.py:29
  112.4 5.4 %fusion.68 = (bf16[128,16384]{1,0:T(8,128)(2,1)}, bf16[128,16384]{1,0:T(8,128)(2,1)}) fusion(f32[8,16,16384]{2,1,0:T(8,128)S(1)} %get-tuple-element.234, f32[8,16,16384]{2,1,0:T(8,128)S(1)} %get-tuple-element.235, f32[16384]{0:T(1024)S(1)} %bitcast.62, f32[16384]{0:T(1024)S(1)} %bitcast.61), kind=kLoop, calls=%fused_computation.10.clone.1 | loop fusion | flops 18874368 | bytes 25296896 | tf_op jit(solution)/shard_map/convert.4
  117.8 4.1 %fusion.65 = (f32[16,16384]{1,0:T(8,128)S(1)}, f32[16,16384]{1,0:T(8,128)S(1)}) fusion(s32[16384]{0:T(1024)S(1)} %bitcast.56), kind=kLoop, calls=%fused_computation.59.clone.1 | loop fusion | flops 3670016 | bytes 2162688 | tf_op jit(solution)/shard_map/while/body/eval_jaxpr/cos | solution.py:16
  121.9 4.2 %subtract_convert_fusion.2 = (bf16[8,16,16384]{2,1,0:T(8,128)(2,1)}, bf16[8,16,16384]{2,1,0:T(8,128)(2,1)}) fusion(f32[16,16384]{1,0:T(8,128)S(1)} %get-tuple-element.219, f32[8,16384]{1,0:T(8,128)S(1)} %get-tuple-element.225, f32[16,16384]{1,0:T(8,128)S(1)} %get-tuple-element.226, f32[8,16384]{1,0:T(8,128)S(1)} %get-tuple-element.227), kind=kLoop, calls=%fused_computation.17.clone.1 | loop fusion | flops 16777216 | bytes 11534336 | tf_op jit(solution)/shard_map/convert.3
  126.1 8.2 %fusion.69 = f32[128,128]{1,0:T(8,128)S(1)} fusion(bf16[128,16384]{1,0:T(8,128)(2,1)} %bitcast.53, bf16[128,16384]{1,0:T(8,128)(2,1)} %bitcast.52, bf16[128,16384]{1,0:T(8,128)(2,1)} %get-tuple-element.238, bf16[128,16384]{1,0:T(8,128)(2,1)} %get-tuple-element.239, f32[128,128]{1,0:T(8,128)S(1)} %get-tuple-element.252, pred[]{:T(512)S(6)} %compare.15), kind=kOutput, calls=%fused_computation.48.clone.1 | convolution fusion | flops 1107329024 | bytes 16908288 | tf_op jit(solution)/shard_map/while/body/eval_jaxpr/dot_general | solution.py:49
  134.4 0.3 dynamic-slice_multiply_fusion.3
  134.7 0.5 fusion.66
  135.2 4.3 %multiply_subtract_fusion.5 = (f32[8,16384]{1,0:T(8,128)S(1)}, f32[8,16384]{1,0:T(8,128)S(1)}, f32[8,16384]{1,0:T(8,128)S(1)}, f32[8,16384]{1,0:T(8,128)S(1)}) fusion(f32[16384]{0:T(1024)S(1)} %get-tuple-element.221, s32[16384]{0:T(1024)S(1)} %bitcast.58, s32[8]{0:T(128)S(1)} %iota_multiply_fusion.2, f32[16384]{0:T(1024)S(1)} %get-tuple-element.222, ...), kind=kLoop, calls=%fused_computation.62.clone.1 | loop fusion | flops 5242880 | bytes 2490400 | tf_op jit(solution)/shard_map/while/body/eval_jaxpr/sub | solution.py:26
  139.5 4.1 %fusion.67 = (f32[16,16384]{1,0:T(8,128)S(1)}, f32[16,16384]{1,0:T(8,128)S(1)}) fusion(s32[16384]{0:T(1024)S(1)} %bitcast.59), kind=kLoop, calls=%fused_computation.61.clone.1 | loop fusion | flops 3670016 | bytes 2162688 | tf_op jit(solution)/shard_map/while/body/eval_jaxpr/cos | solution.py:16
  143.6 2.3 %multiply_subtract_fusion.6 = (f32[8,16,16384]{2,1,0:T(8,128)S(1)}, f32[8,16,16384]{2,1,0:T(8,128)S(1)}) fusion(f32[16,16384]{1,0:T(8,128)S(1)} %get-tuple-element.230, f32[8,16384]{1,0:T(8,128)S(1)} %get-tuple-element.231, f32[16,16384]{1,0:T(8,128)S(1)} %get-tuple-element.232, f32[8,16384]{1,0:T(8,128)S(1)} %get-tuple-element.233), kind=kLoop, calls=%fused_computation.19.clone.1 | loop fusion | flops 12582912 | bytes 19922944 | tf_op jit(solution)/shard_map/while/body/eval_jaxpr/sub | solution.py:29
  145.9 5.4 %fusion.68 = (bf16[128,16384]{1,0:T(8,128)(2,1)}, bf16[128,16384]{1,0:T(8,128)(2,1)}) fusion(f32[8,16,16384]{2,1,0:T(8,128)S(1)} %get-tuple-element.234, f32[8,16,16384]{2,1,0:T(8,128)S(1)} %get-tuple-element.235, f32[16384]{0:T(1024)S(1)} %bitcast.62, f32[16384]{0:T(1024)S(1)} %bitcast.61), kind=kLoop, calls=%fused_computation.10.clone.1 | loop fusion | flops 18874368 | bytes 25296896 | tf_op jit(solution)/shard_map/convert.4
  151.4 4.1 %fusion.65 = (f32[16,16384]{1,0:T(8,128)S(1)}, f32[16,16384]{1,0:T(8,128)S(1)}) fusion(s32[16384]{0:T(1024)S(1)} %bitcast.56), kind=kLoop, calls=%fused_computation.59.clone.1 | loop fusion | flops 3670016 | bytes 2162688 | tf_op jit(solution)/shard_map/while/body/eval_jaxpr/cos | solution.py:16
  155.4 4.2 %subtract_convert_fusion.2 = (bf16[8,16,16384]{2,1,0:T(8,128)(2,1)}, bf16[8,16,16384]{2,1,0:T(8,128)(2,1)}) fusion(f32[16,16384]{1,0:T(8,128)S(1)} %get-tuple-element.219, f32[8,16384]{1,0:T(8,128)S(1)} %get-tuple-element.225, f32[16,16384]{1,0:T(8,128)S(1)} %get-tuple-element.226, f32[8,16384]{1,0:T(8,128)S(1)} %get-tuple-element.227), kind=kLoop, calls=%fused_computation.17.clone.1 | loop fusion | flops 16777216 | bytes 11534336 | tf_op jit(solution)/shard_map/convert.3
  159.7 8.2 %fusion.69 = f32[128,128]{1,0:T(8,128)S(1)} fusion(bf16[128,16384]{1,0:T(8,128)(2,1)} %bitcast.53, bf16[128,16384]{1,0:T(8,128)(2,1)} %bitcast.52, bf16[128,16384]{1,0:T(8,128)(2,1)} %get-tuple-element.238, bf16[128,16384]{1,0:T(8,128)(2,1)} %get-tuple-element.239, f32[128,128]{1,0:T(8,128)S(1)} %get-tuple-element.252, pred[]{:T(512)S(6)} %compare.15), kind=kOutput, calls=%fused_computation.48.clone.1 | convolution fusion | flops 1107329024 | bytes 16908288 | tf_op jit(solution)/shard_map/while/body/eval_jaxpr/dot_general | solution.py:49
  167.9 0.0 copy-start
  167.9 0.6 copy-done
  168.5 0.0 reduce-scatter.2.cloned.1.call-update
  168.5 26.3 %reduce-scatter.2.cloned.1.call-done = f32[32,128]{1,0:T(8,128)} async-done(((f32[128,128]{1,0:T(8,128)}), f32[32,128]{1,0:T(8,128)}) %reduce-scatter.2.cloned.1.call-update) | async-done | bytes 16400 | tf_op jit(solution)/shard_map/reduce_scatter | solution.py:86
  194.8 1.3 multiply_bitcast_fusion
  (4 shorter events, 0.0 us)
Async XLA Ops:
  6.5 188.3 %reduce-scatter.2.cloned.1.call-start = ((), (), s32[]{:S(2)}) async-start(), calls=%async_computation.1 | async-start | bytes 81920 | tf_op jit(solution)/shard_map/reduce_scatter | solution.py:86
  167.9 0.6 copy-start
Sparse Core Ops, SparseCore 0:
  168.7 26.1 reduce-scatter.1
where the time goes:
time: 203 us
  blocking collectives  88.1 us (43%)
  other arithmetic  55.2 us (27%)
  waiting for transfers between devices  26.3 us (13%)
  matrix products  16.4 us (8%)
  between operations  14.7 us (7%)
  local copies, waits for them, and re-layouts  2.13 us (1%)
    all_gather x1, blocking collectives, body(): lax.all_gather(packed, 'facet', axis=0, tiled=True)  88.1 us
    reduce_scatter x1, waiting for transfers between devices, body(): share = lax.psum_scatter(image, 'freq', scatter_dimension=0, tiled=True)  26.3 us
    another operation x4, other arithmetic  19.3 us
    cos x6, other arithmetic, angle_table(): return (jnp.cos(turns), jnp.sin(turns))  17.3 us
    dot_general x2, matrix products, facet_image(): lax.dot_general(left, right, (((1,), (1,)), ((), ())), preferred_element_...  16.4 us
    sub x2, other arithmetic, phase_table(): outer_cos = base_cos * coarse_cos - base_sin * coarse_sin  8.67 us
    sub x2, other arithmetic, phase_table(): outer_cos[:, None, :] * fine_cos[None, :, :]  4.64 us
  transfers between devices with their start and end apart: 1, of which 1 were waited for; matrix products, arithmetic and copies ran while one was open for 0% of the time, Pallas kernels for 0%

commit v1 on v0

--- a/solution.py
+++ b/solution.py
@@ -79,7 +79,12 @@
     facet_col = facets[0, 0]
     facet_row = facets[0, 1]
     image = slab_image(
-        flatten_blocks(lax.all_gather(packed, "facet", axis=0, tiled=True), gains),
+        flatten_blocks(
+            jnp.concatenate(
+                lax.all_to_all(jnp.stack([packed] * lax.axis_size("facet")), "facet", 0, 0), axis=0
+            ),
+            gains,
+        ),
         facet_col,
         facet_row,
     )

time: 203 us -> 128 us (0.63)
  blocking collectives: 88.1 us -> 0 us
  starting transfers between devices: 0.01 us -> 11.2 us
  local copies, waits for them, and re-layouts: 2.13 us -> 4.64 us
    all_gather x1 -> x0, blocking collectives: 88.1 us -> none  [body(): lax.all_gather(packed, 'facet', axis=0, tiled=True)]
    reduce_scatter x1, waiting for transfers between devices: 26.3 us -> 14.6 us  [body(): share = lax.psum_scatter(image, 'freq', scatter_dimension=0, tiled=True)]
    all_to_all x0 -> x1, starting transfers between devices: none -> 11.2 us  [body(): lax.all_to_all(jnp.stack([packed] * lax.axis_size('facet')), 'facet', 0, 0)]
    all_to_all x0 -> x1, waiting for transfers between devices: none -> 10.7 us  [body(): lax.all_to_all(jnp.stack([packed] * lax.axis_size('facet')), 'facet', 0, 0)]
  transfers between devices with their start and end apart: 1 -> 2, of which waited for: 1 -> 2; matrix products, arithmetic and copies ran while one was open for 0% -> 2% of each run, Pallas kernels for 0% -> 0%
where the time goes in v1:
time: 128 us; the launch traced here: 127 us
  other arithmetic  54.8 us (43%)
  waiting for transfers between devices  25.2 us (20%)
  matrix products  16.4 us (13%)
  between operations  14.8 us (12%)
  starting transfers between devices  11.2 us (9%)
  local copies, waits for them, and re-layouts  4.64 us (4%)
    another operation x4, other arithmetic  19.3 us
    cos x6, other arithmetic, angle_table(): return (jnp.cos(turns), jnp.sin(turns))  17.3 us
    dot_general x2, matrix products, facet_image(): lax.dot_general(left, right, (((1,), (1,)), ((), ())), preferred_element_...  16.4 us
    reduce_scatter x1, waiting for transfers between devices, body(): share = lax.psum_scatter(image, 'freq', scatter_dimension=0, tiled=True)  14.6 us
    all_to_all x1, starting transfers between devices, body(): lax.all_to_all(jnp.stack([packed] * lax.axis_size('facet')), 'facet', 0, 0)  11.2 us
    all_to_all x1, waiting for transfers between devices, body(): lax.all_to_all(jnp.stack([packed] * lax.axis_size('facet')), 'facet', 0, 0)  10.7 us
    sub x2, other arithmetic, phase_table(): outer_cos = base_cos * coarse_cos - base_sin * coarse_sin  8.67 us
    sub x2, other arithmetic, phase_table(): outer_cos[:, None, :] * fine_cos[None, :, :]  4.64 us
  transfers between devices with their start and end apart: 2, of which 2 were waited for; matrix products, arithmetic and copies ran while one was open for 2% of the time, Pallas kernels for 0%

profile of v1, /device:TPU:1, one launch (start us, length us, event | category | flops | bytes accessed | tf_op | source)
XLA Modules:
  0.0 127.4 jit_solution(11489990757071709084)
XLA Ops:
  6.5 0.7 convert_element_type.174
  7.2 0.7 multiply_bitcast_fusion.1
  8.0 0.7 pad_maximum_fusion
  8.7 1.0 stack.2
  9.7 11.2 %all-to-all-start = ((f32[32,2,5,512]{3,1,2,0:T(2,128)}), f32[32,2,5,512]{3,1,2,0:T(2,128)S(1)}, u32[]{:S(2)}, u32[]{:S(2)}) async-start(f32[32,2,5,512]{3,1,2,0:T(2,128)} %stack.2), calls=%async_computation | async-start | bytes 1310720 | tf_op jit(solution)/shard_map/all_to_all | solution.py:84
  20.9 0.0 reduce-scatter.2.cloned.1.call-start
  20.9 1.3 %fusion.55 = (s32[1,1]{1,0:T(1,128)}, s32[1,1]{1,0:T(1,128)}) fusion(s32[1,2]{1,0:T(1,128)} %param.15), kind=kLoop, calls=%fused_computation.98 | loop fusion | bytes 16 | tf_op jit(solution)/shard_map/slice | solution.py:80
  23.5 0.8 select_reduce_fusion
  24.3 10.7 %all-to-all-done = f32[32,2,5,512]{3,1,2,0:T(2,128)S(1)} async-done(((f32[32,2,5,512]{3,1,2,0:T(2,128)}), f32[32,2,5,512]{3,1,2,0:T(2,128)S(1)}, u32[]{:S(2)}, u32[]{:S(2)}) %all-to-all-start) | async-done | bytes 655392 | tf_op jit(solution)/shard_map/all_to_all | solution.py:84
  35.0 0.2 copy.17
  35.2 0.5 reshape.566
  35.7 0.1 slice_multiply_fusion
  35.9 0.6 reshape_reshape.3
  36.4 0.4 copy.20
  36.8 67.2 %while.14 = (s32[]{:T(128)}, f32[128,128]{1,0:T(8,128)S(1)}, f32[2,5,16384]{2,1,0:T(8,128)S(1)}, s32[]{:T(128)}, s32[]{:T(128)}, /*index=5*/s32[]{:T(128)}, s32[]{:T(128)}, s32[]{}, s32[]{}, s32[]{}, /*index=10*/s32[]{}) while((s32[]{:T(128)}, f32[128,128]{1,0:T(8,128)S(1)}, f32[2,5,16384]{2,1,0:T(8,128)S(1)}, s32[]{:T(128)}, ...), condition=%wide.region_2.3_spmd.clone, body=%wide.region_1.2_spmd.clone.sunk | while | flops 1168670720 | bytes 81461504 | solution.py:61
  37.0 0.3 dynamic-slice_multiply_fusion.3
  37.3 0.5 fusion.66
  37.8 4.3 %multiply_subtract_fusion.5 = (f32[8,16384]{1,0:T(8,128)S(1)}, f32[8,16384]{1,0:T(8,128)S(1)}, f32[8,16384]{1,0:T(8,128)S(1)}, f32[8,16384]{1,0:T(8,128)S(1)}) fusion(f32[16384]{0:T(1024)S(1)} %get-tuple-element.221, s32[16384]{0:T(1024)S(1)} %bitcast.62, s32[8]{0:T(128)S(1)} %iota_multiply_fusion.2, f32[16384]{0:T(1024)S(1)} %get-tuple-element.222, ...), kind=kLoop, calls=%fused_computation.62.clone.1 | loop fusion | flops 5242880 | bytes 2490400 | tf_op jit(solution)/shard_map/while/body/eval_jaxpr/sub | solution.py:26
  42.2 4.1 %fusion.67 = (f32[16,16384]{1,0:T(8,128)S(1)}, f32[16,16384]{1,0:T(8,128)S(1)}) fusion(s32[16384]{0:T(1024)S(1)} %bitcast.63), kind=kLoop, calls=%fused_computation.61.clone.1 | loop fusion | flops 3670016 | bytes 2162688 | tf_op jit(solution)/shard_map/while/body/eval_jaxpr/cos | solution.py:16
  46.2 2.3 %multiply_subtract_fusion.6 = (f32[8,16,16384]{2,1,0:T(8,128)S(1)}, f32[8,16,16384]{2,1,0:T(8,128)S(1)}) fusion(f32[16,16384]{1,0:T(8,128)S(1)} %get-tuple-element.230, f32[8,16384]{1,0:T(8,128)S(1)} %get-tuple-element.231, f32[16,16384]{1,0:T(8,128)S(1)} %get-tuple-element.232, f32[8,16384]{1,0:T(8,128)S(1)} %get-tuple-element.233), kind=kLoop, calls=%fused_computation.19.clone.1 | loop fusion | flops 12582912 | bytes 19922944 | tf_op jit(solution)/shard_map/while/body/eval_jaxpr/sub | solution.py:29
  48.6 5.4 %fusion.68 = (bf16[128,16384]{1,0:T(8,128)(2,1)}, bf16[128,16384]{1,0:T(8,128)(2,1)}) fusion(f32[8,16,16384]{2,1,0:T(8,128)S(1)} %get-tuple-element.234, f32[8,16,16384]{2,1,0:T(8,128)S(1)} %get-tuple-element.235, f32[16384]{0:T(1024)S(1)} %bitcast.66, f32[16384]{0:T(1024)S(1)} %bitcast.65), kind=kLoop, calls=%fused_computation.10.clone.1 | loop fusion | flops 18874368 | bytes 25296896 | tf_op jit(solution)/shard_map/convert.4
  54.0 4.1 %fusion.65 = (f32[16,16384]{1,0:T(8,128)S(1)}, f32[16,16384]{1,0:T(8,128)S(1)}) fusion(s32[16384]{0:T(1024)S(1)} %bitcast.60), kind=kLoop, calls=%fused_computation.59.clone.1 | loop fusion | flops 3670016 | bytes 2162688 | tf_op jit(solution)/shard_map/while/body/eval_jaxpr/cos | solution.py:16
  58.1 4.2 %subtract_convert_fusion.2 = (bf16[8,16,16384]{2,1,0:T(8,128)(2,1)}, bf16[8,16,16384]{2,1,0:T(8,128)(2,1)}) fusion(f32[16,16384]{1,0:T(8,128)S(1)} %get-tuple-element.219, f32[8,16384]{1,0:T(8,128)S(1)} %get-tuple-element.225, f32[16,16384]{1,0:T(8,128)S(1)} %get-tuple-element.226, f32[8,16384]{1,0:T(8,128)S(1)} %get-tuple-element.227), kind=kLoop, calls=%fused_computation.17.clone.1 | loop fusion | flops 16777216 | bytes 11534336 | tf_op jit(solution)/shard_map/convert.3
  62.3 8.2 %fusion.69 = f32[128,128]{1,0:T(8,128)S(1)} fusion(bf16[128,16384]{1,0:T(8,128)(2,1)} %bitcast.57, bf16[128,16384]{1,0:T(8,128)(2,1)} %bitcast.56, bf16[128,16384]{1,0:T(8,128)(2,1)} %get-tuple-element.238, bf16[128,16384]{1,0:T(8,128)(2,1)} %get-tuple-element.239, f32[128,128]{1,0:T(8,128)S(1)} %get-tuple-element.252, pred[]{:T(512)S(6)} %compare.15), kind=kOutput, calls=%fused_computation.48.clone.1 | convolution fusion | flops 1107329024 | bytes 16908288 | tf_op jit(solution)/shard_map/while/body/eval_jaxpr/dot_general | solution.py:49
  70.5 0.3 dynamic-slice_multiply_fusion.3
  70.8 0.5 fusion.66
  71.3 4.3 %multiply_subtract_fusion.5 = (f32[8,16384]{1,0:T(8,128)S(1)}, f32[8,16384]{1,0:T(8,128)S(1)}, f32[8,16384]{1,0:T(8,128)S(1)}, f32[8,16384]{1,0:T(8,128)S(1)}) fusion(f32[16384]{0:T(1024)S(1)} %get-tuple-element.221, s32[16384]{0:T(1024)S(1)} %bitcast.62, s32[8]{0:T(128)S(1)} %iota_multiply_fusion.2, f32[16384]{0:T(1024)S(1)} %get-tuple-element.222, ...), kind=kLoop, calls=%fused_computation.62.clone.1 | loop fusion | flops 5242880 | bytes 2490400 | tf_op jit(solution)/shard_map/while/body/eval_jaxpr/sub | solution.py:26
  75.7 4.1 %fusion.67 = (f32[16,16384]{1,0:T(8,128)S(1)}, f32[16,16384]{1,0:T(8,128)S(1)}) fusion(s32[16384]{0:T(1024)S(1)} %bitcast.63), kind=kLoop, calls=%fused_computation.61.clone.1 | loop fusion | flops 3670016 | bytes 2162688 | tf_op jit(solution)/shard_map/while/body/eval_jaxpr/cos | solution.py:16
  79.8 2.3 %multiply_subtract_fusion.6 = (f32[8,16,16384]{2,1,0:T(8,128)S(1)}, f32[8,16,16384]{2,1,0:T(8,128)S(1)}) fusion(f32[16,16384]{1,0:T(8,128)S(1)} %get-tuple-element.230, f32[8,16384]{1,0:T(8,128)S(1)} %get-tuple-element.231, f32[16,16384]{1,0:T(8,128)S(1)} %get-tuple-element.232, f32[8,16384]{1,0:T(8,128)S(1)} %get-tuple-element.233), kind=kLoop, calls=%fused_computation.19.clone.1 | loop fusion | flops 12582912 | bytes 19922944 | tf_op jit(solution)/shard_map/while/body/eval_jaxpr/sub | solution.py:29
  82.1 5.4 %fusion.68 = (bf16[128,16384]{1,0:T(8,128)(2,1)}, bf16[128,16384]{1,0:T(8,128)(2,1)}) fusion(f32[8,16,16384]{2,1,0:T(8,128)S(1)} %get-tuple-element.234, f32[8,16,16384]{2,1,0:T(8,128)S(1)} %get-tuple-element.235, f32[16384]{0:T(1024)S(1)} %bitcast.66, f32[16384]{0:T(1024)S(1)} %bitcast.65), kind=kLoop, calls=%fused_computation.10.clone.1 | loop fusion | flops 18874368 | bytes 25296896 | tf_op jit(solution)/shard_map/convert.4
  87.5 4.1 %fusion.65 = (f32[16,16384]{1,0:T(8,128)S(1)}, f32[16,16384]{1,0:T(8,128)S(1)}) fusion(s32[16384]{0:T(1024)S(1)} %bitcast.60), kind=kLoop, calls=%fused_computation.59.clone.1 | loop fusion | flops 3670016 | bytes 2162688 | tf_op jit(solution)/shard_map/while/body/eval_jaxpr/cos | solution.py:16
  91.6 4.2 %subtract_convert_fusion.2 = (bf16[8,16,16384]{2,1,0:T(8,128)(2,1)}, bf16[8,16,16384]{2,1,0:T(8,128)(2,1)}) fusion(f32[16,16384]{1,0:T(8,128)S(1)} %get-tuple-element.219, f32[8,16384]{1,0:T(8,128)S(1)} %get-tuple-element.225, f32[16,16384]{1,0:T(8,128)S(1)} %get-tuple-element.226, f32[8,16384]{1,0:T(8,128)S(1)} %get-tuple-element.227), kind=kLoop, calls=%fused_computation.17.clone.1 | loop fusion | flops 16777216 | bytes 11534336 | tf_op jit(solution)/shard_map/convert.3
  95.8 8.2 %fusion.69 = f32[128,128]{1,0:T(8,128)S(1)} fusion(bf16[128,16384]{1,0:T(8,128)(2,1)} %bitcast.57, bf16[128,16384]{1,0:T(8,128)(2,1)} %bitcast.56, bf16[128,16384]{1,0:T(8,128)(2,1)} %get-tuple-element.238, bf16[128,16384]{1,0:T(8,128)(2,1)} %get-tuple-element.239, f32[128,128]{1,0:T(8,128)S(1)} %get-tuple-element.252, pred[]{:T(512)S(6)} %compare.15), kind=kOutput, calls=%fused_computation.48.clone.1 | convolution fusion | flops 1107329024 | bytes 16908288 | tf_op jit(solution)/shard_map/while/body/eval_jaxpr/dot_general | solution.py:49
  104.0 0.0 copy-start
  104.1 0.6 copy-done
  104.7 0.0 reduce-scatter.2.cloned.1.call-update
  104.7 14.6 %reduce-scatter.2.cloned.1.call-done = f32[32,128]{1,0:T(8,128)} async-done(((f32[128,128]{1,0:T(8,128)}), f32[32,128]{1,0:T(8,128)}) %reduce-scatter.2.cloned.1.call-update) | async-done | bytes 16400 | tf_op jit(solution)/shard_map/reduce_scatter | solution.py:91
  119.2 1.3 %multiply_bitcast_fusion = f32[1,32,128]{2,1,0:T(8,128)} fusion(f32[32,128]{1,0:T(8,128)} %reduce-scatter.2.cloned.1.call-done), kind=kLoop, calls=%fused_computation.95 | loop fusion | flops 4096 | bytes 32768 | tf_op jit(solution)/shard_map/broadcast_in_dim | solution.py:93
  (7 shorter events, 0.1 us)
Async XLA Ops:
  9.7 25.3 %all-to-all-start = ((f32[32,2,5,512]{3,1,2,0:T(2,128)}), f32[32,2,5,512]{3,1,2,0:T(2,128)S(1)}, u32[]{:S(2)}, u32[]{:S(2)}) async-start(f32[32,2,5,512]{3,1,2,0:T(2,128)} %stack.2), calls=%async_computation | async-start | bytes 1310720 | tf_op jit(solution)/shard_map/all_to_all | solution.py:84
  20.9 98.4 %reduce-scatter.2.cloned.1.call-start = ((), (), s32[]{:S(2)}) async-start(), calls=%async_computation.2 | async-start | bytes 81920 | tf_op jit(solution)/shard_map/reduce_scatter | solution.py:91
  104.0 0.6 copy-start
Sparse Core Ops, SparseCore 0:
  104.8 14.3 reduce-scatter.1
